TPU v7x, 512 devices: a whole 4x8x8 slice. The times are simulated.
512 devices in a mesh: seq: 64 (over x, y, core), head: 8 (over z).
Axes of the slice: x: 4, y: 8, z: 8, core: 2. Of those that a mesh axis runs over, the one named last changes fastest.
Arguments:
- queries: bfloat16 [69632, 2048], P('seq', 'head'), may hold values from -50 to 50
- keys: bfloat16 [69632, 2048], P('seq', 'head'), may hold values from -6 to 6
- values: bfloat16 [69632, 2048], P('seq', 'head'), may hold values from -48 to 48
- rand_group: int32 [1088, 3], replicated, may hold values from 0 to 63, all different within a row; in each aligned block of 17 rows (0 to 16, 17 to 33, ...) at most 2 rows name the same one
- rand_offset: int32 [1088, 3], replicated, may hold values from 0 to 16
- glob_blocks: int32 [2], replicated, may hold values from 0 to 1087
- w_out: bfloat16 [2048, 4096], P(None, 'head'), may hold values from -0.125 to 0.125
Outputs:
- layer_out: bfloat16 [69632, 4096], P('seq', 'head')
Inputs may be any that keep to these rules, and one draw needn't show every extreme that they name: `rand_group`: each row names 3 different groups. Among the 17 rows of one aligned block of 17 rows, no group is named more than 2 times, and in every draw some group is named exactly 2 times in some such block.
All inputs are finite; a program needn't handle non-finite values.
Results may differ from a plain program's by a relative error of at most 0.0056.
Values may be sent and summed in bfloat16 or wider, within the bound.
A program may use at most 128 MiB of HBM per device.

v0:
```python
from functools import reduce
import math
import jax
import jax.numpy as jnp
from jax import lax
from jax.sharding import PartitionSpec as P

DH = 128
BLOCK = 64
R = 3
G = 2


def padded_2(x, sides, width):
    for axis, dim in sides:
        size, length = (lax.axis_size(axis), x.shape[dim])
        up = [(i, (i + 1) % size) for i in range(size)]
        down = [(j, i) for i, j in up]
        last = lax.slice_in_dim(x, length - width, length, axis=dim)
        initial = lax.slice_in_dim(x, 0, width, axis=dim)
        before = lax.ppermute(last, axis, up)
        after = lax.ppermute(initial, axis, down)
        x = jnp.concatenate([before, x, after], axis=dim)
    return x


def spread(block, axis, holder):
    block = jnp.where(lax.axis_index(axis) == holder, block, jnp.zeros_like(block))
    return lax.psum(block, axis)


def attend_sets(query_rows, pair_sets, columns):
    head_count = columns // DH
    block_count = query_rows.shape[0]
    query_heads = query_rows.reshape(block_count, BLOCK, head_count, DH)
    score_scale = 1.0 / math.sqrt(DH)
    score_list = []
    for pair_rows in pair_sets:
        key_part = pair_rows[..., :columns].reshape(block_count, -1, head_count, DH)
        score_list.append(
            jnp.einsum("nqhd,nkhd->nhqk", query_heads, key_part, preferred_element_type=jnp.float32)
            * score_scale
        )
    row_max = reduce(
        jnp.maximum, [jnp.max(score_part, axis=-1, keepdims=True) for score_part in score_list]
    )
    row_total = jnp.zeros((block_count, head_count, BLOCK), jnp.float32)
    weighted = jnp.zeros((block_count, BLOCK, head_count, DH), jnp.float32)
    for score_part, pair_rows in zip(score_list, pair_sets):
        weights = jnp.exp(score_part - row_max)
        row_total = jnp.sum(weights, axis=-1)
        value_part = pair_rows[..., columns:].reshape(block_count, -1, head_count, DH)
        weighted = jnp.einsum(
            "nhqk,nkhd->nqhd",
            weights.astype(jnp.bfloat16),
            value_part,
            preferred_element_type=jnp.float32,
        )
    context = weighted / jnp.transpose(row_total, (0, 2, 1))[..., None]
    return context.astype(jnp.bfloat16).reshape(block_count * BLOCK, columns)


def on_device(queries, keys, values, rand_group, rand_offset, glob_blocks, w_out):
    columns = queries.shape[1]
    tokens_dev = queries.shape[0]
    per_device = tokens_dev // BLOCK
    seq_count = lax.axis_size("seq")
    my_index = lax.axis_index("seq")
    slot_cap = rand_group.shape[0] // seq_count * R
    slot_cap = max(2, (slot_cap + seq_count - 1) // seq_count)
    pair_rows = jnp.concatenate([keys, values], axis=1)
    pair_blocks = pair_rows.reshape(per_device, BLOCK, 2 * columns)
    padded = padded_2(pair_rows, (("seq", 0),), BLOCK)
    padded_blocks = padded.reshape(per_device + 2, BLOCK, 2 * columns)
    window_sets = jnp.stack([padded_blocks[:-2], padded_blocks[1:-1], padded_blocks[2:]], axis=1)
    found = []
    for global_slot in range(G):
        owner_index = glob_blocks[global_slot] // per_device
        local_spot = glob_blocks[global_slot] % per_device
        piece_rows = lax.dynamic_index_in_dim(pair_blocks, local_spot, 0, keepdims=False)
        found.append(spread(piece_rows, "seq", owner_index))
    global_pairs = jnp.stack(found)
    global_sets = jnp.broadcast_to(global_pairs[None], (per_device, G, BLOCK, 2 * columns))
    request_count = per_device * R
    asked_groups = rand_group.reshape(seq_count, request_count)
    asked_offsets = rand_offset.reshape(seq_count, request_count)
    asked_here = (asked_groups == my_index).astype(jnp.int32)
    slot_rank = jnp.cumsum(asked_here, axis=1) - asked_here
    slot_index = jnp.arange(slot_cap, dtype=jnp.int32)
    slot_match = (asked_here[:, None, :] == 1) & (
        slot_rank[:, None, :] == slot_index[None, :, None]
    )
    send_spot = jnp.sum(jnp.where(slot_match, asked_offsets[:, None, :], 0), axis=2)
    slot_filled = jnp.any(slot_match, axis=2)
    outgoing = jnp.take(pair_blocks, send_spot.reshape(-1), axis=0).reshape(
        seq_count, slot_cap, BLOCK, 2 * columns
    )
    outgoing = jnp.where(slot_filled[:, :, None, None], outgoing, jnp.zeros_like(outgoing))
    incoming = lax.all_to_all(outgoing, "seq", split_axis=0, concat_axis=0, tiled=True)
    my_groups = lax.dynamic_slice_in_dim(rand_group, my_index * per_device, per_device, 0).reshape(
        -1
    )
    request_index = jnp.arange(request_count, dtype=jnp.int32)
    earlier_same = (my_groups[None, :] == my_groups[:, None]) & (
        request_index[None, :] < request_index[:, None]
    )
    arrival_rank = jnp.sum(earlier_same.astype(jnp.int32), axis=1)
    arrival_spot = my_groups * slot_cap + arrival_rank
    random_sets = jnp.take(
        incoming.reshape(seq_count * slot_cap, BLOCK, 2 * columns), arrival_spot, axis=0
    )
    random_sets = random_sets.reshape(per_device, R, BLOCK, 2 * columns)
    query_rows = queries.reshape(per_device, BLOCK, columns)
    joined_sets = jnp.concatenate([window_sets, global_sets, random_sets], axis=1).reshape(
        per_device, -1, 2 * columns
    )
    context = attend_sets(query_rows, [joined_sets], columns)
    summed = jnp.dot(
        lax.all_gather(context, "head", axis=1, tiled=True),
        w_out,
        preferred_element_type=jnp.float32,
    )
    return summed.astype(jnp.bfloat16)


def solution(mesh):
    return jax.shard_map(
        on_device,
        mesh=mesh,
        in_specs=(
            P("seq", "head"),
            P("seq", "head"),
            P("seq", "head"),
            P(),
            P(),
            P(),
            P(None, "head"),
        ),
        out_specs=P("seq", "head"),
        check_vma=False,
    )
```

profile of v0, /device:TPU:64, one launch (start us, length us, event | category | flops | bytes accessed | tf_op | source)
XLA Modules:
  0.0 396.6 jit_solution(1737452305502771908)
XLA Ops:
  6.5 0.9 compare_convert_fusion
  7.4 0.2 copy.53
  8.3 1.0 copy.58
  9.8 1.1 constant_dynamic-update-slice_fusion.1
  11.3 1.1 constant_dynamic-update-slice_fusion
  12.4 6.4 %gather_fusion = bf16[128,64,512]{2,1,0:T(8,128)(2,1)} fusion(bf16[17,64,512]{2,1,0:T(8,128)(2,1)S(1)} %bitcast.52, s32[1024]{0:T(1024)S(1)} %pad_clamp_fusion.1), kind=kCustom, calls=%fused_computation | custom fusion | bytes 16777728 | tf_op jit(solution)/shard_map/jit(_take)/gather | solution.py:95
  18.8 7.5 %select_select_fusion = bf16[64,2,64,512]{3,2,1,0:T(8,128)(2,1)} fusion(bf16[64,2,64,512]{3,2,1,0:T(8,128)(2,1)} %bitcast.55, pred[64,2]{1,0:T(8,128)(4,1)S(1)} %copy.60, pred[64,2]{1,0:T(8,128)(4,1)S(1)} %copy.57), kind=kLoop, calls=%fused_computation.2 | loop fusion | flops 8388608 | bytes 16777472 | tf_op jit(solution)/shard_map/jit(_where)/select_n | solution.py:98
  26.3 10.9 %all-to-all-start = ((bf16[64,2,64,512]{3,2,1,0:T(8,128)(2,1)}), bf16[64,2,64,512]{3,2,1,0:T(8,128)(2,1)}, u32[]{:S(2)}, u32[]{:S(2)}) async-start(bf16[64,2,64,512]{3,2,1,0:T(8,128)(2,1)} %select_select_fusion), calls=%async_computation | async-start | bytes 16777216 | tf_op jit(solution)/shard_map/all_to_all | solution.py:99
  37.3 1.9 collective-permute-start
  39.2 7.0 %collective-permute-start.1 = (bf16[64,512]{1,0:T(8,128)(2,1)S(1)}, bf16[64,512]{1,0:T(8,128)(2,1)S(1)}, u32[]{:S(2)}, u32[]{:S(2)}) collective-permute-start(bf16[64,512]{1,0:T(8,128)(2,1)S(1)} %get-tuple-element.15), channel_id=1, source_target_pairs={{8,0},{16,8},{24,16},{32,24},{40,32},{48,40},{56,48},{64,56},{72,6... | collective-permute-start | bytes 196616 | tf_op jit(solution)/shard_map/ppermute | solution.py:22
  46.2 0.6 fusion.21
  50.5 0.7 dynamic-slice_select_fusion.1
  51.4 0.8 broadcast_multiply_fusion
  53.0 2.5 reshape_reshape.3
  55.5 213.7 %all-reduce.3.cloned.1.call-done = (bf16[1,64,512]{2,1,0:T(8,128)(2,1)}, bf16[1,64,512]{2,1,0:T(8,128)(2,1)}) async-done(((bf16[1,64,512]{2,1,0:T(8,128)(2,1)}, bf16[1,64,512]{2,1,0:T(8,128)(2,1)}), (bf16[1,64,512]{2,1,0:T(8,128)(2,1)}, bf16[1,64,512]{2,1,0:T(8,128)(2,1)})) %all-reduce.3.cloned.1.call-update) | async-done | bytes 131088 | tf_op jit(solution)/shard_map/psum | solution.py:29
  269.2 0.9 pad_maximum_fusion.2
  270.3 1.1 constant_dynamic-update-slice_fusion.4
  271.4 1.1 constant_dynamic-update-slice_fusion.3
  272.4 1.1 constant_dynamic-update-slice_fusion.2
  273.5 1.7 broadcast_dynamic-update-slice_fusion
  275.2 5.9 %gather_fusion.1 = bf16[51,64,512]{2,1,0:T(8,128)(2,1)} fusion(bf16[128,64,512]{2,1,0:T(8,128)(2,1)} %bitcast.12, s32[1024]{0:T(1024)S(1)} %pad_clamp_fusion), kind=kCustom, calls=%fused_computation.1 | custom fusion | bytes 6684876 | tf_op jit(solution)/shard_map/jit(_take)/gather | solution.py:109
  281.1 5.2 %select_dynamic-update-slice_fusion = bf16[17,8,64,512]{3,2,1,0:T(8,128)(2,1)} fusion(bf16[17,8,64,512]{3,2,1,0:T(8,128)(2,1)} %broadcast_dynamic-update-slice_fusion, bf16[17,3,64,512]{3,2,1,0:T(8,128)(2,1)} %bitcast.57, pred[17,3]{1,0:T(8,128)(4,1)S(1)} %copy.52), kind=kLoop, calls=%fused_computation.8 | loop fusion | flops 1671168 | bytes 6684723 | tf_op jit(solution)/shard_map/concatenate | solution.py:114
  286.2 8.1 %fusion.19 = (bf16[17,512,256]{2,1,0:T(8,128)(2,1)}, bf16[17,512,256]{2,1,0:T(8,128)(2,1)}) fusion(bf16[17,512,512]{2,1,0:T(8,128)(2,1)} %bitcast.16), kind=kLoop, calls=%fused_computation.51 | loop fusion | bytes 17825792 | tf_op jit(solution)/shard_map/slice | solution.py:39
  294.3 6.5 %copy.64 = bf16[17,512,256]{1,2,0:T(8,128)(2,1)} copy(bf16[17,512,256]{2,1,0:T(8,128)(2,1)} %get-tuple-element.9) | data formatting | bytes 8912896 | tf_op jit(solution)/shard_map/slice | solution.py:39
  300.8 6.6 %copy.63 = bf16[17,512,256]{1,2,0:T(8,128)(2,1)} copy(bf16[17,512,256]{2,1,0:T(8,128)(2,1)} %get-tuple-element.10) | data formatting | bytes 8912896 | tf_op jit(solution)/shard_map/slice | solution.py:52
  307.5 3.4 bitcast_reduce_fusion
  310.9 1.3 fusion.1
  312.2 2.0 divide_convert_fusion
  314.3 0.6 copy.68
  314.8 0.9 copy.78
  315.8 68.3 %all-gather.2.cloned.1.call-done = bf16[1088,2048]{1,0:T(8,128)(2,1)} async-done(((bf16[1088,256]{1,0:T(8,128)(2,1)}), bf16[1088,2048]{1,0:T(8,128)(2,1)}) %all-gather.2.cloned.1.call-update) | async-done | bytes 4456464 | tf_op jit(solution)/shard_map/all_gather | solution.py:119
  384.1 5.7 %convolution_convert_fusion = bf16[1088,512]{1,0:T(8,128)(2,1)} fusion(bf16[1088,2048]{1,0:T(8,128)(2,1)} %all-gather.2.cloned.1.call-done, bf16[2048,512]{1,0:T(8,128)(2,1)S(1)} %copy-done), kind=kOutput, calls=%fused_computation.9 | convolution fusion | flops 2282258432 | bytes 7667712 | tf_op jit(solution)/shard_map/dot_general | solution.py:118
  (48 shorter events, 2.9 us)
Async XLA Ops:
  6.5 377.5 %copy-start = (bf16[2048,512]{1,0:T(8,128)(2,1)S(1)}, bf16[2048,512]{1,0:T(8,128)(2,1)}, u32[]{:S(2)}) copy-start(bf16[2048,512]{1,0:T(8,128)(2,1)} %param.13) | copy-start | bytes 6291460
  26.3 19.9 %copy-start.2 = (s32[2]{0:T(128)S(1)}, s32[2]{0:T(128)}, u32[]{:S(2)}) copy-start(s32[2]{0:T(128)} %param.12) | copy-start | bytes 28
  26.3 248.9 %all-to-all-start = ((bf16[64,2,64,512]{3,2,1,0:T(8,128)(2,1)}), bf16[64,2,64,512]{3,2,1,0:T(8,128)(2,1)}, u32[]{:S(2)}, u32[]{:S(2)}) async-start(bf16[64,2,64,512]{3,2,1,0:T(8,128)(2,1)} %select_select_fusion), calls=%async_computation | async-start | bytes 16777216 | tf_op jit(solution)/shard_map/all_to_all | solution.py:99
  37.2 232.0 %all-reduce.3.cloned.1.call-start = ((), (), s32[]{:S(2)}) async-start(), calls=%async_computation.2 | async-start | bytes 262144 | tf_op jit(solution)/shard_map/psum | solution.py:29
  37.3 232.8 %collective-permute-start = (bf16[64,512]{1,0:T(8,128)(2,1)S(1)}, bf16[64,512]{1,0:T(8,128)(2,1)S(1)}, u32[]{:S(2)}, u32[]{:S(2)}) collective-permute-start(bf16[64,512]{1,0:T(8,128)(2,1)S(1)} %get-tuple-element.16), channel_id=1, source_target_pairs={{0,8},{8,16},{16,24},{24,32},{32,40},{40,48},{48,56},{56,64},{64,7... | collective-permute-start | bytes 196616 | tf_op jit(solution)/shard_map/ppermute | solution.py:21
  39.2 230.9 %collective-permute-start.1 = (bf16[64,512]{1,0:T(8,128)(2,1)S(1)}, bf16[64,512]{1,0:T(8,128)(2,1)S(1)}, u32[]{:S(2)}, u32[]{:S(2)}) collective-permute-start(bf16[64,512]{1,0:T(8,128)(2,1)S(1)} %get-tuple-element.15), channel_id=1, source_target_pairs={{8,0},{16,8},{24,16},{32,24},{40,32},{48,40},{56,48},{64,56},{72,6... | collective-permute-start | bytes 196616 | tf_op jit(solution)/shard_map/ppermute | solution.py:22
  51.2 332.9 %all-gather.2.cloned.1.call-start = ((), (), s32[]{:S(2)}) async-start(), calls=%async_computation.1 | async-start | bytes 5013504 | tf_op jit(solution)/shard_map/all_gather | solution.py:119
  300.8 6.6 %copy-start.1 = (bf16[17,64,2,128]{3,2,1,0:T(2,128)(2,1)S(1)}, bf16[17,64,2,128]{3,2,1,0:T(2,128)(2,1)}, u32[]{:S(2)}) copy-start(bf16[17,64,2,128]{3,2,1,0:T(2,128)(2,1)} %reshape_reshape.3) | copy-start | bytes 1671172
  307.4 4.8 %slice-start = ((s8[4456448]{0:T(1024)(128)(4,1)}), s8[4194304]{0:T(1024)(128)(4,1)S(1)}, s32[]{:S(2)}) async-start(s8[4456448]{0:T(1024)(128)(4,1)} %bitcast.58), calls=%async_computation.3 | async-start | bytes 8388608
  307.5 4.8 %slice-start.1 = ((s8[4456448]{0:T(1024)(128)(4,1)}), s8[262144]{0:T(1024)(128)(4,1)S(1)}, s32[]{:S(2)}) async-start(s8[4456448]{0:T(1024)(128)(4,1)} %bitcast.58), calls=%async_computation.4 | async-start | bytes 524288
Sparse Core Ops, SparseCore 0:
  51.3 217.8 all-reduce.2
  315.9 68.1 all-gather.1
where the time goes:
time: 398 us; the launch traced here: 397 us
  waiting for transfers between devices  282 us (71%)
  local copies, waits for them, and re-layouts  48.1 us (12%)
  starting transfers between devices  20.1 us (5%)
  other arithmetic  17.9 us (4%)
  between operations  17.3 us (4%)
  matrix products  11.2 us (3%)
    psum x1, waiting for transfers between devices, spread(): return lax.psum(block, axis)  214 us
    all_gather x1, waiting for transfers between devices, on_device(): lax.all_gather(context, 'head', axis=1, tiled=True)  68.3 us
    slice x2, local copies, waits for them, and re-layouts, attend_sets(): key_part = pair_rows[..., :columns].reshape(block_count, -1, head_count, DH)  14.6 us
    all_to_all x1, starting transfers between devices, on_device(): lax.all_to_all(outgoing, 'seq', split_axis=0, concat_axis=0, tiled=True)  10.9 us
  transfers between devices with their start and end apart: 5, of which 2 were waited for; matrix products, arithmetic and copies ran while one was open for 3% of the time, Pallas kernels for 0%

commit v1 on v0

--- a/solution.py
+++ b/solution.py
@@ -9,6 +9,24 @@
 BLOCK = 64
 R = 3
 G = 2
+
+
+def gather_around(shard, axis, dim):
+    ways, here, hop = (lax.axis_size(axis), lax.axis_index(axis), shard.shape[dim])
+    lengths = [n * ways if d == dim else n for d, n in enumerate(shard.shape)]
+    full = lax.dynamic_update_slice_in_dim(
+        jnp.zeros(lengths, shard.dtype), shard, here * hop, axis=dim
+    )
+    going_up = going_down = shard
+    for far in range(1, ways // 2 + 1):
+        going_up = lax.ppermute(going_up, axis, [(d, (d + 1) % ways) for d in range(ways)])
+        full = lax.dynamic_update_slice_in_dim(full, going_up, (here - far) % ways * hop, axis=dim)
+        if 2 * far < ways:
+            going_down = lax.ppermute(going_down, axis, [(d, (d - 1) % ways) for d in range(ways)])
+            full = lax.dynamic_update_slice_in_dim(
+                full, going_down, (here + far) % ways * hop, axis=dim
+            )
+    return full
 
 
 def padded_2(x, sides, width):
@@ -115,11 +133,7 @@
         per_device, -1, 2 * columns
     )
     context = attend_sets(query_rows, [joined_sets], columns)
-    summed = jnp.dot(
-        lax.all_gather(context, "head", axis=1, tiled=True),
-        w_out,
-        preferred_element_type=jnp.float32,
-    )
+    summed = jnp.dot(gather_around(context, "head", 1), w_out, preferred_element_type=jnp.float32)
     return summed.astype(jnp.bfloat16)
 
 

time: 398 us -> 398 us (level)
  the two profiles are of different devices: /device:TPU:64 before, /device:TPU:2 now
where the time goes in v1:
time: 398 us; the launch traced here: 397 us
  waiting for transfers between devices  258 us (65%)
  local copies, waits for them, and re-layouts  51.8 us (13%)
  starting transfers between devices  42.8 us (11%)
  other arithmetic  17.9 us (4%)
  between operations  17.8 us (4%)
  matrix products  8.89 us (2%)
    psum x1, waiting for transfers between devices, spread(): return lax.psum(block, axis)  215 us
    ppermute x4, waiting for transfers between devices, gather_around(): lax.ppermute(going_up, axis, [(d, (d + 1) % ways) for d in range(ways)])  41.3 us
    slice x2, local copies, waits for them, and re-layouts, attend_sets(): key_part = pair_rows[..., :columns].reshape(block_count, -1, head_count, DH)  14.6 us
    ppermute x3, starting transfers between devices, gather_around(): lax.ppermute(going_down, axis, [(d, (d - 1) % ways) for d in range(ways)])  14.5 us
    all_to_all x1, starting transfers between devices, on_device(): lax.all_to_all(outgoing, 'seq', split_axis=0, concat_axis=0, tiled=True)  11.1 us
    ppermute x4, starting transfers between devices, gather_around(): lax.ppermute(going_up, axis, [(d, (d + 1) % ways) for d in range(ways)])  9.29 us
  transfers between devices with their start and end apart: 11, of which 7 were waited for; matrix products, arithmetic and copies ran while one was open for 4% of the time, Pallas kernels for 0%

profile of v1, /device:TPU:2, one launch (start us, length us, event | category | flops | bytes accessed | tf_op | source)
XLA Modules:
  0.0 396.6 jit_solution(11217484784528925267)
XLA Ops:
  12.4 6.6 %gather_fusion = bf16[128,64,512]{2,1,0:T(8,128)(2,1)} fusion(bf16[17,64,512]{2,1,0:T(8,128)(2,1)S(1)} %bitcast.54, s32[1024]{0:T(1024)S(1)} %pad_clamp_fusion.1), kind=kCustom, calls=%fused_computation | custom fusion | bytes 16777728 | tf_op jit(solution)/shard_map/jit(_take)/gather | solution.py:113
  19.0 7.5 %select_select_fusion = bf16[64,2,64,512]{3,2,1,0:T(8,128)(2,1)} fusion(bf16[64,2,64,512]{3,2,1,0:T(8,128)(2,1)} %bitcast.57, pred[64,2]{1,0:T(8,128)(4,1)S(1)} %copy.60, pred[64,2]{1,0:T(8,128)(4,1)S(1)} %copy.57), kind=kLoop, calls=%fused_computation.2 | loop fusion | flops 8388608 | bytes 16777472 | tf_op jit(solution)/shard_map/jit(_where)/select_n | solution.py:116
  26.5 11.1 %all-to-all-start = ((bf16[64,2,64,512]{3,2,1,0:T(8,128)(2,1)}), bf16[64,2,64,512]{3,2,1,0:T(8,128)(2,1)}, u32[]{:S(2)}, u32[]{:S(2)}) async-start(bf16[64,2,64,512]{3,2,1,0:T(8,128)(2,1)} %select_select_fusion), calls=%async_computation | async-start | bytes 16777216 | tf_op jit(solution)/shard_map/all_to_all | solution.py:117
  37.7 2.1 collective-permute-start
  39.7 5.8 %collective-permute-start.1 = (bf16[64,512]{1,0:T(8,128)(2,1)S(1)}, bf16[64,512]{1,0:T(8,128)(2,1)S(1)}, u32[]{:S(2)}, u32[]{:S(2)}) collective-permute-start(bf16[64,512]{1,0:T(8,128)(2,1)S(1)} %get-tuple-element.15), channel_id=1, source_target_pairs={{8,0},{16,8},{24,16},{32,24},{40,32},{48,40},{56,48},{64,56},{72,6... | collective-permute-start | bytes 196616 | tf_op jit(solution)/shard_map/ppermute | solution.py:40
  52.4 2.5 reshape_reshape.3
  54.9 214.9 %all-reduce.3.cloned.1.call-done = (bf16[1,64,512]{2,1,0:T(8,128)(2,1)}, bf16[1,64,512]{2,1,0:T(8,128)(2,1)}) async-done(((bf16[1,64,512]{2,1,0:T(8,128)(2,1)}, bf16[1,64,512]{2,1,0:T(8,128)(2,1)}), (bf16[1,64,512]{2,1,0:T(8,128)(2,1)}, bf16[1,64,512]{2,1,0:T(8,128)(2,1)})) %all-reduce.3.cloned.1.call-update) | async-done | bytes 131088 | tf_op jit(solution)/shard_map/psum | solution.py:47
  274.1 1.6 broadcast_dynamic-update-slice_fusion
  275.7 5.9 %gather_fusion.1 = bf16[51,64,512]{2,1,0:T(8,128)(2,1)} fusion(bf16[128,64,512]{2,1,0:T(8,128)(2,1)} %bitcast.12, s32[1024]{0:T(1024)S(1)} %pad_clamp_fusion), kind=kCustom, calls=%fused_computation.1 | custom fusion | bytes 6684876 | tf_op jit(solution)/shard_map/jit(_take)/gather | solution.py:127
  281.6 5.1 %select_dynamic-update-slice_fusion = bf16[17,8,64,512]{3,2,1,0:T(8,128)(2,1)} fusion(bf16[17,8,64,512]{3,2,1,0:T(8,128)(2,1)} %broadcast_dynamic-update-slice_fusion, bf16[17,3,64,512]{3,2,1,0:T(8,128)(2,1)} %bitcast.59, pred[17,3]{1,0:T(8,128)(4,1)S(1)} %copy.52), kind=kLoop, calls=%fused_computation.8 | loop fusion | flops 1671168 | bytes 6684723 | tf_op jit(solution)/shard_map/concatenate | solution.py:132
  286.7 8.1 %fusion.19 = (bf16[17,512,256]{2,1,0:T(8,128)(2,1)}, bf16[17,512,256]{2,1,0:T(8,128)(2,1)}) fusion(bf16[17,512,512]{2,1,0:T(8,128)(2,1)} %bitcast.16), kind=kLoop, calls=%fused_computation.59 | loop fusion | bytes 17825792 | tf_op jit(solution)/shard_map/slice | solution.py:57
  294.8 6.5 %copy.64 = bf16[17,512,256]{1,2,0:T(8,128)(2,1)} copy(bf16[17,512,256]{2,1,0:T(8,128)(2,1)} %get-tuple-element.9) | data formatting | bytes 8912896 | tf_op jit(solution)/shard_map/slice | solution.py:57
  301.3 6.6 %copy.63 = bf16[17,512,256]{1,2,0:T(8,128)(2,1)} copy(bf16[17,512,256]{2,1,0:T(8,128)(2,1)} %get-tuple-element.10) | data formatting | bytes 8912896 | tf_op jit(solution)/shard_map/slice | solution.py:70
  307.9 3.4 bitcast_reduce_fusion
  311.3 1.3 fusion.1
  312.7 2.0 divide_convert_fusion
  315.4 3.6 collective-permute-start.2
  319.0 4.2 %collective-permute-start.3 = (bf16[1088,256]{1,0:T(8,128)(2,1)S(1)}, bf16[1088,256]{1,0:T(8,128)(2,1)}, u32[]{:S(2)}, u32[]{:S(2)}) collective-permute-start(bf16[1088,256]{1,0:T(8,128)(2,1)S(1)} %bitcast.68), channel_id=1, source_target_pairs={{0,7},{1,0},{2,1},{3,2},{4,3},{5,4},{6,5},{7,6},{8,15},{9,8},{10,9... | collective-permute-start | bytes 1671176 | tf_op jit(solution)/shard_map/ppermute | solution.py:25
  323.2 11.1 %collective-permute-done.2 = bf16[1088,256]{1,0:T(8,128)(2,1)} collective-permute-done((bf16[1088,256]{1,0:T(8,128)(2,1)S(1)}, bf16[1088,256]{1,0:T(8,128)(2,1)}, u32[]{:S(2)}, u32[]{:S(2)}) %collective-permute-start.2) | collective-permute-done | bytes 557088 | tf_op jit(solution)/shard_map/ppermute | solution.py:22
  334.3 1.9 collective-permute-start.4
  336.4 5.1 %collective-permute-start.5 = (bf16[1088,256]{1,0:T(8,128)(2,1)}, bf16[1088,256]{1,0:T(8,128)(2,1)S(1)}, u32[]{:S(2)}, u32[]{:S(2)}) collective-permute-start(bf16[1088,256]{1,0:T(8,128)(2,1)} %collective-permute-done.3), channel_id=1, source_target_pairs={{0,7},{1,0},{2,1},{3,2},{4,3},{5,4},{6,5},{7,6},{8,15},{9,8},{10,9... | collective-permute-start | bytes 1671176 | tf_op jit(solution)/shard_map/ppermute | solution.py:25
  342.3 10.3 %collective-permute-done.4 = bf16[1088,256]{1,0:T(8,128)(2,1)} collective-permute-done((bf16[1088,256]{1,0:T(8,128)(2,1)}, bf16[1088,256]{1,0:T(8,128)(2,1)}, u32[]{:S(2)}, u32[]{:S(2)}) %collective-permute-start.4) | collective-permute-done | bytes 557088 | tf_op jit(solution)/shard_map/ppermute | solution.py:22
  352.6 1.9 collective-permute-start.6
  354.5 1.1 constant_dynamic-update-slice_fusion.10
  355.6 1.1 constant_dynamic-update-slice_fusion.9
  356.8 5.1 %collective-permute-start.7 = (bf16[1088,256]{1,0:T(8,128)(2,1)S(1)}, bf16[1088,256]{1,0:T(8,128)(2,1)S(1)}, u32[]{:S(2)}, u32[]{:S(2)}) collective-permute-start(bf16[1088,256]{1,0:T(8,128)(2,1)S(1)} %collective-permute-done.5), channel_id=1, source_target_pairs={{0,7},{1,0},{2,1},{3,2},{4,3},{5,4},{6,5},{7,6},{8,15},{9,8},{10,9... | collective-permute-start | bytes 1671176 | tf_op jit(solution)/shard_map/ppermute | solution.py:25
  361.9 1.1 constant_dynamic-update-slice_fusion.8
  363.1 6.9 %collective-permute-done.6 = bf16[1088,256]{1,0:T(8,128)(2,1)S(1)} collective-permute-done((bf16[1088,256]{1,0:T(8,128)(2,1)}, bf16[1088,256]{1,0:T(8,128)(2,1)S(1)}, u32[]{:S(2)}, u32[]{:S(2)}) %collective-permute-start.6) | collective-permute-done | bytes 557088 | tf_op jit(solution)/shard_map/ppermute | solution.py:22
  370.0 1.9 collective-permute-start.8
  372.1 1.2 collective-permute-done.7
  373.3 12.9 %collective-permute-done.8 = bf16[1088,256]{1,0:T(8,128)(2,1)S(1)} collective-permute-done((bf16[1088,256]{1,0:T(8,128)(2,1)S(1)}, bf16[1088,256]{1,0:T(8,128)(2,1)S(1)}, u32[]{:S(2)}, u32[]{:S(2)}) %collective-permute-start.8) | collective-permute-done | bytes 557088 | tf_op jit(solution)/shard_map/ppermute | solution.py:22
  386.3 3.5 convolution_convert_fusion
  (68 shorter events, 14.8 us)
Async XLA Ops:
  6.5 379.8 %copy-start = (bf16[2048,512]{1,0:T(8,128)(2,1)S(1)}, bf16[2048,512]{1,0:T(8,128)(2,1)}, u32[]{:S(2)}) copy-start(bf16[2048,512]{1,0:T(8,128)(2,1)} %param.13) | copy-start | bytes 6291460
  26.5 19.0 %copy-start.2 = (s32[2]{0:T(128)S(1)}, s32[2]{0:T(128)}, u32[]{:S(2)}) copy-start(s32[2]{0:T(128)} %param.12) | copy-start | bytes 28
  26.5 249.2 %all-to-all-start = ((bf16[64,2,64,512]{3,2,1,0:T(8,128)(2,1)}), bf16[64,2,64,512]{3,2,1,0:T(8,128)(2,1)}, u32[]{:S(2)}, u32[]{:S(2)}) async-start(bf16[64,2,64,512]{3,2,1,0:T(8,128)(2,1)} %select_select_fusion), calls=%async_computation | async-start | bytes 16777216 | tf_op jit(solution)/shard_map/all_to_all | solution.py:117
  37.6 232.2 %all-reduce.3.cloned.1.call-start = ((), (), s32[]{:S(2)}) async-start(), calls=%async_computation.1 | async-start | bytes 262144 | tf_op jit(solution)/shard_map/psum | solution.py:47
  37.7 233.0 %collective-permute-start = (bf16[64,512]{1,0:T(8,128)(2,1)S(1)}, bf16[64,512]{1,0:T(8,128)(2,1)S(1)}, u32[]{:S(2)}, u32[]{:S(2)}) collective-permute-start(bf16[64,512]{1,0:T(8,128)(2,1)S(1)} %get-tuple-element.16), channel_id=1, source_target_pairs={{0,8},{8,16},{16,24},{24,32},{32,40},{40,48},{48,56},{56,64},{64,7... | collective-permute-start | bytes 196616 | tf_op jit(solution)/shard_map/ppermute | solution.py:39
  39.7 231.0 %collective-permute-start.1 = (bf16[64,512]{1,0:T(8,128)(2,1)S(1)}, bf16[64,512]{1,0:T(8,128)(2,1)S(1)}, u32[]{:S(2)}, u32[]{:S(2)}) collective-permute-start(bf16[64,512]{1,0:T(8,128)(2,1)S(1)} %get-tuple-element.15), channel_id=1, source_target_pairs={{8,0},{16,8},{24,16},{32,24},{40,32},{48,40},{56,48},{64,56},{72,6... | collective-permute-start | bytes 196616 | tf_op jit(solution)/shard_map/ppermute | solution.py:40
  301.3 6.7 %copy-start.1 = (bf16[17,64,2,128]{3,2,1,0:T(2,128)(2,1)S(1)}, bf16[17,64,2,128]{3,2,1,0:T(2,128)(2,1)}, u32[]{:S(2)}) copy-start(bf16[17,64,2,128]{3,2,1,0:T(2,128)(2,1)} %reshape_reshape.3) | copy-start | bytes 1671172
  307.9 4.8 %slice-start = ((s8[4456448]{0:T(1024)(128)(4,1)}), s8[4194304]{0:T(1024)(128)(4,1)S(1)}, s32[]{:S(2)}) async-start(s8[4456448]{0:T(1024)(128)(4,1)} %bitcast.62), calls=%async_computation.2 | async-start | bytes 8388608
  307.9 4.8 %slice-start.1 = ((s8[4456448]{0:T(1024)(128)(4,1)}), s8[262144]{0:T(1024)(128)(4,1)S(1)}, s32[]{:S(2)}) async-start(s8[4456448]{0:T(1024)(128)(4,1)} %bitcast.62), calls=%async_computation.3 | async-start | bytes 524288
  315.4 18.9 %collective-permute-start.2 = (bf16[1088,256]{1,0:T(8,128)(2,1)S(1)}, bf16[1088,256]{1,0:T(8,128)(2,1)}, u32[]{:S(2)}, u32[]{:S(2)}) collective-permute-start(bf16[1088,256]{1,0:T(8,128)(2,1)S(1)} %bitcast.67), channel_id=1, source_target_pairs={{0,1},{1,2},{2,3},{3,4},{4,5},{5,6},{6,7},{7,0},{8,9},{9,10},{10,1... | collective-permute-start | bytes 1671176 | tf_op jit(solution)/shard_map/ppermute | solution.py:22
  319.0 17.5 %collective-permute-start.3 = (bf16[1088,256]{1,0:T(8,128)(2,1)S(1)}, bf16[1088,256]{1,0:T(8,128)(2,1)}, u32[]{:S(2)}, u32[]{:S(2)}) collective-permute-start(bf16[1088,256]{1,0:T(8,128)(2,1)S(1)} %bitcast.68), channel_id=1, source_target_pairs={{0,7},{1,0},{2,1},{3,2},{4,3},{5,4},{6,5},{7,6},{8,15},{9,8},{10,9... | collective-permute-start | bytes 1671176 | tf_op jit(solution)/shard_map/ppermute | solution.py:25
  334.3 18.3 %collective-permute-start.4 = (bf16[1088,256]{1,0:T(8,128)(2,1)}, bf16[1088,256]{1,0:T(8,128)(2,1)}, u32[]{:S(2)}, u32[]{:S(2)}) collective-permute-start(bf16[1088,256]{1,0:T(8,128)(2,1)} %collective-permute-done.2), channel_id=1, source_target_pairs={{0,1},{1,2},{2,3},{3,4},{4,5},{5,6},{6,7},{7,0},{8,9},{9,10},{10,1... | collective-permute-start | bytes 1671176 | tf_op jit(solution)/shard_map/ppermute | solution.py:22
  336.4 20.3 %collective-permute-start.5 = (bf16[1088,256]{1,0:T(8,128)(2,1)}, bf16[1088,256]{1,0:T(8,128)(2,1)S(1)}, u32[]{:S(2)}, u32[]{:S(2)}) collective-permute-start(bf16[1088,256]{1,0:T(8,128)(2,1)} %collective-permute-done.3), channel_id=1, source_target_pairs={{0,7},{1,0},{2,1},{3,2},{4,3},{5,4},{6,5},{7,6},{8,15},{9,8},{10,9... | collective-permute-start | bytes 1671176 | tf_op jit(solution)/shard_map/ppermute | solution.py:25
  352.6 17.4 %collective-permute-start.6 = (bf16[1088,256]{1,0:T(8,128)(2,1)}, bf16[1088,256]{1,0:T(8,128)(2,1)S(1)}, u32[]{:S(2)}, u32[]{:S(2)}) collective-permute-start(bf16[1088,256]{1,0:T(8,128)(2,1)} %collective-permute-done.4), channel_id=1, source_target_pairs={{0,1},{1,2},{2,3},{3,4},{4,5},{5,6},{6,7},{7,0},{8,9},{9,10},{10,1... | collective-permute-start | bytes 1671176 | tf_op jit(solution)/shard_map/ppermute | solution.py:22
  356.8 16.4 %collective-permute-start.7 = (bf16[1088,256]{1,0:T(8,128)(2,1)S(1)}, bf16[1088,256]{1,0:T(8,128)(2,1)S(1)}, u32[]{:S(2)}, u32[]{:S(2)}) collective-permute-start(bf16[1088,256]{1,0:T(8,128)(2,1)S(1)} %collective-permute-done.5), channel_id=1, source_target_pairs={{0,7},{1,0},{2,1},{3,2},{4,3},{5,4},{6,5},{7,6},{8,15},{9,8},{10,9... | collective-permute-start | bytes 1671176 | tf_op jit(solution)/shard_map/ppermute | solution.py:25
  370.0 16.3 %collective-permute-start.8 = (bf16[1088,256]{1,0:T(8,128)(2,1)S(1)}, bf16[1088,256]{1,0:T(8,128)(2,1)S(1)}, u32[]{:S(2)}, u32[]{:S(2)}) collective-permute-start(bf16[1088,256]{1,0:T(8,128)(2,1)S(1)} %collective-permute-done.6), channel_id=1, source_target_pairs={{0,1},{1,2},{2,3},{3,4},{4,5},{5,6},{6,7},{7,0},{8,9},{9,10},{10,1... | collective-permute-start | bytes 1671176 | tf_op jit(solution)/shard_map/ppermute | solution.py:22
Sparse Core Ops, SparseCore 0:
  50.9 218.8 all-reduce.2
